TPU v7x, 32 devices: a whole 2x2x4 slice. The times are simulated.
32 devices in a mesh: group: 4 (over y, x), expert: 8 (over z, core).
Axes of the slice: x: 2, y: 2, z: 4, core: 2. Of those that a mesh axis runs over, the one named last changes fastest.
Arguments:
- residual_in: bfloat16 [4096, 2560], P(('group', 'expert')), may hold values from -3 to 3
- queries: bfloat16 [4096, 2560], P(('group', 'expert')), may hold values from -8 to 8
- suffix_key_rows: bfloat16 [4096, 512], P(('group', 'expert')), may hold values from -8 to 8
- suffix_value_rows: bfloat16 [4096, 512], P(('group', 'expert')), may hold values from -6 to 6
- cached_prefix_keys: bfloat16 [4096, 512], P(('group', 'expert')), may hold values from -6 to 6
- cached_prefix_values: bfloat16 [4096, 512], P(('group', 'expert')), may hold values from -6 to 6
- suffix_length_list: int32 [4, 8], replicated, may hold values from 1 to 512, 1024 in all within a row
- prefix_read_flags: int32 [4, 8], replicated, may hold values 0 or 1
- attn_out_weight: bfloat16 [2560, 2560], replicated, may hold values from -0.3125 to 0.3125
- norm_gain: float32 [2560], replicated, may hold values from 0.1 to 1.9
- routes: int32 [4096, 6], P(('group', 'expert')), may hold values from 0 to 15, all different within a row; in each aligned block of 128 rows (0 to 127, 128 to 255, ...) at most 64 rows name the same one
- route_weights: float32 [4096, 6], P(('group', 'expert')), may hold values from 0.1 to 1
- expert_gate: bfloat16 [32, 512, 2560], P(('group', 'expert')), may hold values from -0.125 to 0.125
- expert_up: bfloat16 [32, 512, 2560], P(('group', 'expert')), may hold values from -0.125 to 0.125
- expert_down: bfloat16 [32, 512, 2560], P(('group', 'expert')), may hold values from -0.1875 to 0.1875
Outputs:
- layer_out: bfloat16 [4096, 2560], P(('group', 'expert'))
Inputs may be any that keep to these rules, and one draw needn't show every extreme that they name: `suffix_length_list`: the lengths of each group sum to 1024. `routes`: within each aligned block of 128 rows no expert is named by more than 64 rows, and in every draw some block names some expert exactly 64 times.
All inputs are finite; a program needn't handle non-finite values.
Results may differ from a plain program's by a relative error of at most 0.0085.
Values may be sent and summed in bfloat16 or wider, within the bound.
A program may use at most 192 MiB of HBM per device.

v0:
```python
import math

import jax
import jax.numpy as jnp
from jax import lax
from jax.sharding import PartitionSpec as P

QUERY_HEADS = 20
KEY_VALUE_HEADS = 4
HEAD_SIZE = 128
TOP = 6
REQS = 8


def segment_of(positions, bounds):
    return jnp.sum((positions[:, None] >= bounds[None, :]).astype(jnp.int32), axis=1)


def per_device(
    residual_in,
    queries,
    suffix_key_rows,
    suffix_value_rows,
    cached_prefix_keys,
    cached_prefix_values,
    suffix_length_list,
    prefix_read_flags,
    attn_out_weight,
    norm_gain,
    routes,
    route_weights,
    expert_gate,
    expert_up,
    expert_down,
):
    token_rows = queries.shape[0]
    model_width = residual_in.shape[1]
    group_width = QUERY_HEADS // KEY_VALUE_HEADS
    my_group = lax.axis_index("group")
    my_place = lax.axis_index("expert")
    lengths_here = lax.dynamic_index_in_dim(suffix_length_list, my_group, 0, keepdims=False)
    flags_here = lax.dynamic_index_in_dim(prefix_read_flags, my_group, 0, keepdims=False)
    bounds = jnp.cumsum(lengths_here, dtype=jnp.int32)
    query_pos = my_place * token_rows + jnp.arange(token_rows, dtype=jnp.int32)
    query_seg = segment_of(query_pos, bounds)
    request_ids = jnp.arange(REQS, dtype=jnp.int32)
    query_reads = (
        jnp.sum(
            jnp.where(query_seg[:, None] == request_ids[None, :], flags_here[None, :], 0), axis=1
        )
        > 0
    )
    query_head_count = queries.reshape(token_rows, KEY_VALUE_HEADS, group_width, HEAD_SIZE)
    score_scale = 1.0 / math.sqrt(HEAD_SIZE)

    def attend(state_now, pieces, visible):
        running_max, running_sum, weighted = state_now
        key_portion, value_portion = pieces
        count_of_rows = key_portion.shape[0]
        key_row_block = key_portion.reshape(count_of_rows, KEY_VALUE_HEADS, HEAD_SIZE)
        value_row_block = value_portion.reshape(count_of_rows, KEY_VALUE_HEADS, HEAD_SIZE)
        scores = (
            jnp.einsum(
                "tkgd,skd->tkgs",
                query_head_count,
                key_row_block,
                preferred_element_type=jnp.float32,
            )
            * score_scale
        )
        seen = visible[:, None, None, :]
        scores = jnp.where(seen, scores, -jnp.inf)
        new_max = jnp.maximum(running_max, jnp.max(scores, axis=3))
        weights = jnp.where(seen, jnp.exp(scores - new_max[..., None]), 0.0)
        factor = jnp.exp(running_max - new_max)
        running_sum = running_sum * factor + jnp.sum(weights, axis=3)
        weighted = weighted * factor[..., None] + jnp.einsum(
            "tkgs,skd->tkgd",
            weights.astype(jnp.bfloat16),
            value_row_block,
            preferred_element_type=jnp.float32,
        )
        return (new_max, running_sum, weighted)

    start_state = (
        jnp.full((token_rows, KEY_VALUE_HEADS, group_width), -1e30, jnp.float32),
        jnp.zeros((token_rows, KEY_VALUE_HEADS, group_width), jnp.float32),
        jnp.zeros((token_rows, KEY_VALUE_HEADS, group_width, HEAD_SIZE), jnp.float32),
    )
    pieces = (
        lax.all_gather(cached_prefix_keys, "expert", axis=0, tiled=True),
        lax.all_gather(cached_prefix_values, "expert", axis=0, tiled=True),
    )
    visible = jnp.broadcast_to(query_reads[:, None], (token_rows, pieces[0].shape[0]))
    state_now = attend(start_state, pieces, visible)
    pieces = (
        lax.all_gather(suffix_key_rows, "expert", axis=0, tiled=True),
        lax.all_gather(suffix_value_rows, "expert", axis=0, tiled=True),
    )
    key_pos = jnp.arange(pieces[0].shape[0], dtype=jnp.int32)
    key_seg = segment_of(key_pos, bounds)
    visible = (query_seg[:, None] == key_seg[None, :]) & (key_pos[None, :] <= query_pos[:, None])
    state_now = attend(state_now, pieces, visible)
    context = (
        (state_now[2] / state_now[1][..., None])
        .reshape(token_rows, QUERY_HEADS * HEAD_SIZE)
        .astype(jnp.bfloat16)
    )
    hidden = residual_in.astype(jnp.float32) + jnp.dot(
        context, attn_out_weight, preferred_element_type=jnp.float32
    )
    mean_square = jnp.mean(hidden * hidden, axis=1, keepdims=True)
    normed = (hidden * lax.rsqrt(mean_square + 1e-05) * norm_gain).astype(jnp.bfloat16)
    experts = lax.axis_size("group") * lax.axis_size("expert") // 2
    capacity = 2 * ((2 * token_rows * TOP + 3 * experts - 1) // (3 * experts))
    flat_routes = routes.reshape(-1)
    one_hot = (flat_routes[:, None] == jnp.arange(experts, dtype=jnp.int32)[None, :]).astype(
        jnp.int32
    )
    slot_rank = jnp.sum(one_hot * jnp.cumsum(one_hot, axis=0, dtype=jnp.int32), axis=1) - 1
    slot_index = flat_routes * capacity + slot_rank
    slot_ids = jnp.arange(experts * capacity, dtype=jnp.int32)
    dispatch_map = jnp.any(
        slot_index.reshape(token_rows, TOP)[None, :, :] == slot_ids[:, None, None], axis=2
    )
    buffer = jnp.dot(
        dispatch_map.astype(jnp.bfloat16), normed, preferred_element_type=jnp.float32
    ).astype(jnp.bfloat16)
    local_gate = expert_gate[0]
    local_up = expert_up[0]
    local_down = expert_down[0]
    sending = jnp.broadcast_to(
        buffer.reshape(experts, 1, capacity, model_width), (experts, 2, capacity, model_width)
    ).reshape(2 * experts, capacity, model_width)
    arrived = lax.all_to_all(sending, ("group", "expert"), split_axis=0, concat_axis=0, tiled=True)
    gate_act = jnp.einsum("skd,fd->skf", arrived, local_gate, preferred_element_type=jnp.float32)
    up_act = jnp.einsum("skd,fd->skf", arrived, local_up, preferred_element_type=jnp.float32)
    hidden_act = (jax.nn.silu(gate_act) * up_act).astype(jnp.bfloat16)
    returned = lax.all_to_all(
        jnp.einsum(
            "skf,fd->skd", hidden_act, local_down, preferred_element_type=jnp.float32
        ).astype(jnp.bfloat16),
        ("group", "expert"),
        split_axis=0,
        concat_axis=0,
        tiled=True,
    )
    returned = returned.reshape(experts, 2, capacity, model_width)
    results = (returned[:, 0].astype(jnp.float32) + returned[:, 1].astype(jnp.float32)).astype(
        jnp.bfloat16
    )
    results = results.reshape(experts * capacity, model_width)
    chosen = results[slot_index].reshape(token_rows, TOP, model_width)
    norm_weights = route_weights / jnp.sum(route_weights, axis=1, keepdims=True)
    mixed = jnp.einsum("tj,tjd->td", norm_weights, chosen.astype(jnp.float32))
    return (hidden + mixed).astype(jnp.bfloat16)


def solution(mesh):
    in_specs = (
        P(("group", "expert"), None),
        P(("group", "expert"), None),
        P(("group", "expert"), None),
        P(("group", "expert"), None),
        P(("group", "expert"), None),
        P(("group", "expert"), None),
        P(),
        P(),
        P(),
        P(),
        P(("group", "expert"), None),
        P(("group", "expert"), None),
        P(("group", "expert"), None, None),
        P(("group", "expert"), None, None),
        P(("group", "expert"), None, None),
    )
    out_specs = P(("group", "expert"), None)
    return jax.shard_map(
        per_device, mesh=mesh, in_specs=in_specs, out_specs=out_specs, check_vma=False
    )
```

profile of v0, /device:TPU:0, one launch (start us, length us, event | category | flops | bytes accessed | tf_op | source)
XLA Modules:
  0.0 665.3 jit_solution(6561826310800109736)
XLA Ops:
  20.6 15.0 %all-gather.9.cloned.1.call-done = bf16[1024,512]{0,1:T(8,128)(2,1)} async-done(((bf16[128,512]{0,1:T(8,128)(2,1)}), bf16[1024,512]{0,1:T(8,128)(2,1)}) %all-gather.9.cloned.1.call-update) | async-done | bytes 1048592 | tf_op jit(solution)/shard_map/all_gather | solution.py:97
  35.6 7.4 %fusion.2 = (f32[128,4,5]{0,2,1:T(8,128)}, f32[4,1024,128,5]{2,1,3,0:T(8,128)}) fusion(pred[128,1024]{0,1:T(8,128)(4,1)S(1)} %fusion.41, bf16[1024,4,128,1]{0,2,3,1:T(8,128)(2,1)} %bitcast.134, bf16[128,4,5,128]{0,3,2,1:T(8,128)(2,1)S(1)} %bitcast.132), kind=kOutput, calls=%fused_computation.9 | convolution fusion | flops 678950400 | bytes 12331008 | tf_op jit(solution)/shard_map/tkgd,skd->tkgs/dot_general | solution.py:63
  43.0 16.8 %all-gather.5.cloned.1.call-done = bf16[1024,512]{0,1:T(8,128)(2,1)} async-done(((bf16[128,512]{0,1:T(8,128)(2,1)}), bf16[1024,512]{0,1:T(8,128)(2,1)}) %all-gather.5.cloned.1.call-update) | async-done | bytes 1048592 | tf_op jit(solution)/shard_map/all_gather | solution.py:91
  59.9 6.9 %bitcast_reduce_fusion = (f32[128,4,5]{0,2,1:T(8,128)S(1)}, f32[4,1024,128,5]{2,1,3,0:T(8,128)}) fusion(pred[128]{0:T(512)(128)(4,1)} %broadcast_compare_fusion, bf16[1024,4,128,1]{0,2,3,1:T(8,128)(2,1)} %bitcast.136, bf16[128,4,5,128]{0,3,2,1:T(8,128)(2,1)S(1)} %bitcast.133), kind=kOutput, calls=%fused_computation.3 | convolution fusion | flops 678950400 | bytes 12200064 | tf_op jit(solution)/shard_map/tkgd,skd->tkgs/dot_general | solution.py:63
  66.8 2.5 fusion.3
  69.3 12.9 %all-gather.7.cloned.1.call-done = bf16[1024,512]{1,0:T(8,128)(2,1)} async-done(((bf16[128,512]{1,0:T(8,128)(2,1)}), bf16[1024,512]{1,0:T(8,128)(2,1)}) %all-gather.7.cloned.1.call-update) | async-done | bytes 1048592 | tf_op jit(solution)/shard_map/all_gather | solution.py:92
  82.2 2.3 copy.42
  84.5 6.5 fusion.5
  91.6 4.7 fusion.31
  96.3 9.1 %all-gather.11.cloned.1.call-done = bf16[1024,512]{1,0:T(8,128)(2,1)} async-done(((bf16[128,512]{1,0:T(8,128)(2,1)}), bf16[1024,512]{1,0:T(8,128)(2,1)}) %all-gather.11.cloned.1.call-update) | async-done | bytes 1048592 | tf_op jit(solution)/shard_map/all_gather | solution.py:98
  105.4 2.3 copy.47
  107.8 7.4 %divide_convert_fusion = bf16[128,4,5,128]{0,3,2,1:T(8,128)(2,1)S(1)} fusion(f32[128,4,5,128]{0,3,2,1:T(8,128)} %fusion.31, bf16[1024,4,128,1]{0,2,3,1:T(8,128)(2,1)} %bitcast.138, f32[4,1024,128,5]{2,1,3,0:T(8,128)} %get-tuple-element.15, f32[128,4,5]{0,2,1:T(8,128)S(1)} %get-tuple-element.10, pred[128,1024]{0,1:T(8,128)(4,1)S(1)} %fusion.41, ...), kind=kOutput, calls=%fused_computation.38 | convolution fusion | flops 685178880 | bytes 13651968 | tf_op jit(solution)/shard_map/tkgs,skd->tkgd/dot_general | solution.py:77
  118.3 4.0 convolution_convert_fusion.1
  122.3 7.9 %broadcast_in_dim.96 = bf16[16,2,64,2560]{3,2,1,0:T(8,128)(2,1)} broadcast(bf16[16,64,2560]{2,1,0:T(8,128)(2,1)} %bitcast.129), dimensions={0,2,3} | broadcast | bytes 15728640 | tf_op jit(solution)/shard_map/broadcast_in_dim | solution.py:132
  130.2 234.1 %all_to_all.10 = bf16[32,64,2560]{2,1,0:T(8,128)(2,1)S(1)} all-to-all(bf16[32,64,2560]{2,1,0:T(8,128)(2,1)} %bitcast.128), channel_id=1, replica_groups=mesh['group'=4,'expert'=8] {'group','expert'}, dimensions={0} | all-to-all | bytes 20971520 | tf_op jit(solution)/shard_map/all_to_all | solution.py:135
  364.2 3.8 copy-done.5
  368.1 7.3 %fusion.16 = f32[32,64,512]{2,1,0:T(8,128)} fusion(bf16[32,64,2560]{2,1,0:T(8,128)(2,1)S(1)} %all_to_all.10, bf16[1,512,2560]{2,1,0:T(8,128)(2,1)S(1)} %copy-done.15), kind=kOutput, calls=%fused_computation.26 | convolution fusion | flops 5368709120 | bytes 17301504 | tf_op jit(solution)/shard_map/skd,fd->skf/dot_general | solution.py:137
  375.3 17.8 %convolution_convert_fusion = bf16[32,64,2560]{2,1,0:T(8,128)(2,1)} fusion(bf16[1,512,2560]{2,1,0:T(8,128)(2,1)S(1)} %copy-done, f32[32,64,512]{2,1,0:T(8,128)} %fusion.16, bf16[32,64,2560]{2,1,0:T(8,128)(2,1)} %copy-done.5, bf16[1,512,2560]{2,1,0:T(8,128)(2,1)} %param.27), kind=kOutput, calls=%fused_computation.10 | convolution fusion | flops 10748952576 | bytes 30408704 | tf_op jit(solution)/shard_map/skf,fd->skd/dot_general | solution.py:140
  393.2 4.1 all-to-all-start.1
  397.7 229.2 %all-to-all-done.1 = bf16[32,64,2560]{2,1,0:T(8,128)(2,1)} async-done(((bf16[32,64,2560]{2,1,0:T(8,128)(2,1)}), bf16[32,64,2560]{2,1,0:T(8,128)(2,1)}, u32[]{:S(2)}, u32[]{:S(2)}) %all-to-all-start.1) | async-done | bytes 10485792 | tf_op jit(solution)/shard_map/all_to_all | solution.py:139
  626.9 8.0 %add_convert_fusion = bf16[16,1,64,2560]{3,2,1,0:T(8,128)(2,1)} fusion(bf16[16,2,64,2560]{3,2,1,0:T(8,128)(2,1)} %bitcast.29), kind=kLoop, calls=%fused_computation.6 | loop fusion | flops 10485760 | bytes 15728640 | tf_op jit(solution)/shard_map/convert_element_type | solution.py:149
  634.9 11.6 %gather_fusion = bf16[768,2560]{1,0:T(8,128)(2,1)} fusion(bf16[1024,2560]{1,0:T(8,128)(2,1)} %bitcast.127, s32[1024]{0:T(1024)S(1)} %pad_clamp_fusion), kind=kCustom, calls=%fused_computation | custom fusion | bytes 7867392 | tf_op jit(solution)/shard_map/gather | solution.py:153
  646.5 7.1 %reshape.213 = bf16[128,6,2560]{2,1,0:T(8,128)(2,1)} reshape(bf16[768,2560]{1,0:T(8,128)(2,1)} %gather_fusion) | data formatting | bytes 7864320 | tf_op jit(solution)/shard_map/reshape | solution.py:153
  653.7 4.1 fusion.55
  (84 shorter events, 18.9 us)
Async XLA Ops:
  6.5 368.8 %copy-start = (bf16[1,512,2560]{2,1,0:T(8,128)(2,1)S(1)}, bf16[1,512,2560]{2,1,0:T(8,128)(2,1)}, u32[]{:S(2)}) copy-start(bf16[1,512,2560]{2,1,0:T(8,128)(2,1)} %param.29) | copy-start | bytes 7864324
  6.5 29.1 %all-gather.9.cloned.1.call-start = ((), (), s32[]{:S(2)}) async-start(), calls=%async_computation.4 | async-start | bytes 1179648 | tf_op jit(solution)/shard_map/all_gather | solution.py:97
  8.4 51.5 %all-gather.5.cloned.1.call-start = ((), (), s32[]{:S(2)}) async-start(), calls=%async_computation.2 | async-start | bytes 1179648 | tf_op jit(solution)/shard_map/all_gather | solution.py:91
  10.1 72.1 %all-gather.7.cloned.1.call-start = ((), (), s32[]{:S(2)}) async-start(), calls=%async_computation.3 | async-start | bytes 1179648 | tf_op jit(solution)/shard_map/all_gather | solution.py:92
  10.8 94.6 %all-gather.11.cloned.1.call-start = ((), (), s32[]{:S(2)}) async-start(), calls=%async_computation.5 | async-start | bytes 1179648 | tf_op jit(solution)/shard_map/all_gather | solution.py:98
  59.9 6.9 %copy-start.8 = (f32[128,4,5]{0,2,1:T(8,128)S(1)}, f32[128,4,5]{0,2,1:T(8,128)}, u32[]{:S(2)}) copy-start(f32[128,4,5]{0,2,1:T(8,128)} %get-tuple-element.14) | copy-start | bytes 30724
  59.9 7.0 %copy-start.1 = (f32[4,1024,128,5]{2,1,3,0:T(8,128)S(1)}, f32[4,1024,128,5]{2,1,3,0:T(8,128)}, u32[]{:S(2)}) copy-start(f32[4,1024,128,5]{2,1,3,0:T(8,128)} %get-tuple-element.15) | copy-start | bytes 31457284
  66.8 17.7 %copy-start.14 = (pred[128]{0:T(512)(128)(4,1)S(1)}, pred[128]{0:T(512)(128)(4,1)}, u32[]{:S(2)}) copy-start(pred[128]{0:T(512)(128)(4,1)} %broadcast_compare_fusion) | copy-start | bytes 388
  84.5 6.5 copy-start.9
  84.5 7.1 %copy-start.2 = (f32[4,1024,128,5]{2,1,3,0:T(8,128)S(1)}, f32[4,1024,128,5]{2,1,3,0:T(8,128)}, u32[]{:S(2)}) copy-start(f32[4,1024,128,5]{2,1,3,0:T(8,128)} %get-tuple-element.13) | copy-start | bytes 31457284
  105.4 9.8 %slice-start = ((s8[13107200]{0:T(1024)(128)(4,1)}), s8[524288]{0:T(1024)(128)(4,1)S(1)}, s32[]{:S(2)}) async-start(s8[13107200]{0:T(1024)(128)(4,1)} %bitcast.130), calls=%async_computation.6 | async-start | bytes 1048576
  107.7 7.5 %slice-start.1 = ((s8[13107200]{0:T(1024)(128)(4,1)}), s8[4194304]{0:T(1024)(128)(4,1)S(1)}, s32[]{:S(2)}) async-start(s8[13107200]{0:T(1024)(128)(4,1)} %bitcast.130), calls=%async_computation.7 | async-start | bytes 8388608
  107.7 7.5 %slice-start.2 = ((s8[13107200]{0:T(1024)(128)(4,1)}), s8[4194304]{0:T(1024)(128)(4,1)S(1)}, s32[]{:S(2)}) async-start(s8[13107200]{0:T(1024)(128)(4,1)} %bitcast.130), calls=%async_computation.8 | async-start | bytes 8388608
  107.7 8.5 %slice-start.3 = ((s8[13107200]{0:T(1024)(128)(4,1)}), s8[4194304]{0:T(1024)(128)(4,1)S(1)}, s32[]{:S(2)}) async-start(s8[13107200]{0:T(1024)(128)(4,1)} %bitcast.130), calls=%async_computation.9 | async-start | bytes 8388608
  107.7 8.5 %copy-start.6 = (bf16[128,2560]{1,0:T(8,128)(2,1)S(1)}, bf16[128,2560]{1,0:T(8,128)(2,1)}, u32[]{:S(2)}) copy-start(bf16[128,2560]{1,0:T(8,128)(2,1)} %param.15) | copy-start | bytes 1966084
  116.3 2.0 copy-start.13
  118.3 4.0 copy-start.3
  130.2 237.9 %copy-start.15 = (bf16[1,512,2560]{2,1,0:T(8,128)(2,1)S(1)}, bf16[1,512,2560]{2,1,0:T(8,128)(2,1)}, u32[]{:S(2)}) copy-start(bf16[1,512,2560]{2,1,0:T(8,128)(2,1)} %param.28) | copy-start | bytes 7864324
  364.2 3.8 copy-start.5
  393.2 4.2 copy-start.12
  393.2 4.3 copy-start.7
  393.2 4.5 copy-start.11
  393.2 233.7 %all-to-all-start.1 = ((bf16[32,64,2560]{2,1,0:T(8,128)(2,1)}), bf16[32,64,2560]{2,1,0:T(8,128)(2,1)}, u32[]{:S(2)}, u32[]{:S(2)}) async-start(bf16[32,64,2560]{2,1,0:T(8,128)(2,1)} %convolution_convert_fusion), calls=%async_computation.1 | async-start | bytes 20971520 | tf_op jit(solution)/shard_map/all_to_all | solution.py:139
  653.7 4.1 copy-start.4
  (1 other events, 0.6 us)
Sparse Core Ops, SparseCore 0:
  8.9 26.6 all-gather.8
  37.2 22.6 all-gather.4
  61.5 20.6 all-gather.6
  83.7 21.7 all-gather.10
where the time goes:
time: 666 us; the launch traced here: 665 us
  waiting for transfers between devices  284 us (43%)
  blocking collectives  234 us (35%)
  matrix products  61.7 us (9%)
  local copies, waits for them, and re-layouts  45.4 us (7%)
  other arithmetic  22.3 us (3%)
  between operations  13.4 us (2%)
    all_to_all x1, blocking collectives, per_device(): lax.all_to_all(sending, ('group', 'expert'), split_axis=0, concat_axis=0,...  234 us
    all_to_all x1, waiting for transfers between devices, per_device(): lax.all_to_all(jnp.einsum('skf,fd->skd', hidden_act, local_down, preferre...  229 us
    dot_general x1, matrix products, per_device(): jnp.einsum('skf,fd->skd', hidden_act, local_down, preferred_element_type=...  17.8 us
    all_gather x1, waiting for transfers between devices, per_device(): lax.all_gather(cached_prefix_keys, 'expert', axis=0, tiled=True)  16.8 us
    all_gather x1, waiting for transfers between devices, per_device(): lax.all_gather(suffix_key_rows, 'expert', axis=0, tiled=True)  15 us
    dot_general x2, matrix products, attend(): jnp.einsum('tkgd,skd->tkgs', query_head_count, key_row_block, preferred_e...  14.4 us
  transfers between devices with their start and end apart: 5, of which 5 were waited for; matrix products, arithmetic and copies ran while one was open for 6% of the time, Pallas kernels for 0%

commit v1 on v0

--- a/solution.py
+++ b/solution.py
@@ -87,16 +87,23 @@
         jnp.zeros((token_rows, KEY_VALUE_HEADS, group_width), jnp.float32),
         jnp.zeros((token_rows, KEY_VALUE_HEADS, group_width, HEAD_SIZE), jnp.float32),
     )
-    pieces = (
-        lax.all_gather(cached_prefix_keys, "expert", axis=0, tiled=True),
-        lax.all_gather(cached_prefix_values, "expert", axis=0, tiled=True),
-    )
+    key_width = cached_prefix_keys.shape[1]
+    prefix_pair = lax.all_gather(
+        jnp.concatenate([cached_prefix_keys, cached_prefix_values], axis=1),
+        "expert",
+        axis=0,
+        tiled=True,
+    )
+    suffix_pair = lax.all_gather(
+        jnp.concatenate([suffix_key_rows, suffix_value_rows], axis=1),
+        "expert",
+        axis=0,
+        tiled=True,
+    )
+    pieces = (prefix_pair[:, :key_width], prefix_pair[:, key_width:])
     visible = jnp.broadcast_to(query_reads[:, None], (token_rows, pieces[0].shape[0]))
     state_now = attend(start_state, pieces, visible)
-    pieces = (
-        lax.all_gather(suffix_key_rows, "expert", axis=0, tiled=True),
-        lax.all_gather(suffix_value_rows, "expert", axis=0, tiled=True),
-    )
+    pieces = (suffix_pair[:, :key_width], suffix_pair[:, key_width:])
     key_pos = jnp.arange(pieces[0].shape[0], dtype=jnp.int32)
     key_seg = segment_of(key_pos, bounds)
     visible = (query_seg[:, None] == key_seg[None, :]) & (key_pos[None, :] <= query_pos[:, None])
@@ -129,30 +136,52 @@
     local_gate = expert_gate[0]
     local_up = expert_up[0]
     local_down = expert_down[0]
-    sending = jnp.broadcast_to(
-        buffer.reshape(experts, 1, capacity, model_width), (experts, 2, capacity, model_width)
-    ).reshape(2 * experts, capacity, model_width)
+    half_rows = capacity // 2
+    pairs = [(i, i ^ 1) for i in range(lax.axis_size("expert"))]
+
+    def half_expert(rows):
+        gate_act = lax.dot_general(
+            rows, local_gate, (((1,), (1,)), ((), ())), preferred_element_type=jnp.float32
+        )
+        up_act = lax.dot_general(
+            rows, local_up, (((1,), (1,)), ((), ())), preferred_element_type=jnp.float32
+        )
+        hidden_act = (jax.nn.silu(gate_act) * up_act).astype(jnp.bfloat16)
+        return jnp.dot(hidden_act, local_down, preferred_element_type=jnp.float32).astype(
+            jnp.bfloat16
+        )
+
+    sending = buffer.reshape(2 * experts, half_rows, model_width)
     arrived = lax.all_to_all(sending, ("group", "expert"), split_axis=0, concat_axis=0, tiled=True)
-    gate_act = jnp.einsum("skd,fd->skf", arrived, local_gate, preferred_element_type=jnp.float32)
-    up_act = jnp.einsum("skd,fd->skf", arrived, local_up, preferred_element_type=jnp.float32)
-    hidden_act = (jax.nn.silu(gate_act) * up_act).astype(jnp.bfloat16)
-    returned = lax.all_to_all(
-        jnp.einsum(
-            "skf,fd->skd", hidden_act, local_down, preferred_element_type=jnp.float32
-        ).astype(jnp.bfloat16),
+    own_rows = arrived.reshape(2 * experts * half_rows, model_width)
+    pair_rows = lax.ppermute(own_rows, "expert", pairs)
+    partial_pair = half_expert(pair_rows)
+    from_pair = lax.ppermute(partial_pair, "expert", pairs)
+    partial_own = half_expert(own_rows)
+    combined = (partial_own.astype(jnp.float32) + from_pair.astype(jnp.float32)).astype(
+        jnp.bfloat16
+    )
+    results = lax.all_to_all(
+        combined.reshape(2 * experts, half_rows, model_width),
         ("group", "expert"),
         split_axis=0,
         concat_axis=0,
         tiled=True,
-    )
-    returned = returned.reshape(experts, 2, capacity, model_width)
-    results = (returned[:, 0].astype(jnp.float32) + returned[:, 1].astype(jnp.float32)).astype(
-        jnp.bfloat16
-    )
-    results = results.reshape(experts * capacity, model_width)
-    chosen = results[slot_index].reshape(token_rows, TOP, model_width)
+    ).reshape(experts * capacity, model_width)
     norm_weights = route_weights / jnp.sum(route_weights, axis=1, keepdims=True)
-    mixed = jnp.einsum("tj,tjd->td", norm_weights, chosen.astype(jnp.float32))
+    mix_map = jnp.sum(
+        jnp.where(
+            slot_index.reshape(token_rows, TOP)[:, :, None] == slot_ids[None, None, :],
+            norm_weights[:, :, None],
+            0.0,
+        ),
+        axis=1,
+    )
+    mix_high = mix_map.astype(jnp.bfloat16)
+    mix_low = (mix_map - mix_high.astype(jnp.float32)).astype(jnp.bfloat16)
+    mixed = jnp.dot(mix_high, results, preferred_element_type=jnp.float32) + jnp.dot(
+        mix_low, results, preferred_element_type=jnp.float32
+    )
     return (hidden + mixed).astype(jnp.bfloat16)
 
 

time: 666 us -> 404 us (0.61)
  blocking collectives: 234 us -> 121 us
  waiting for transfers between devices: 284 us -> 171 us
  local copies, waits for them, and re-layouts: 45.4 us -> 19.4 us
  other arithmetic: 22.3 us -> 11 us
    all_to_all x1, blocking collectives: 234 us -> 121 us  [per_device(): lax.all_to_all(sending, ('group', 'expert'), split_axis=0, concat_axis=0,...]
    all_to_all x1, waiting for transfers between devices: 229 us -> 117 us  [per_device(): lax.all_to_all(combined.reshape(2 * experts, half_rows, model_width), ('g...]
    dot_general x3 -> x6, matrix products: 29.2 us -> 41.6 us  [the longest x2 22.2 us: half_expert(): jnp.dot(hidden_act, local_down, preferred_element_type=jnp.float32)]
    gather x1 -> x0, local copies, waits for them, and re-layouts: 11.6 us -> none  [per_device(): chosen = results[slot_index].reshape(token_rows, TOP, model_width)]
    ppermute x0 -> x2, waiting for transfers between devices: none -> 10 us  [the longest x1 8.66 us: per_device(): pair_rows = lax.ppermute(own_rows, 'expert', pairs)]
    all_gather x4 -> x2, waiting for transfers between devices: 53.8 us -> 44.4 us  [the longest x1 23.6 us: per_device(): lax.all_gather(jnp.concatenate([cached_prefix_keys, cached_prefix_values]...]
    convert_element_type x2 -> x0, other arithmetic: 8.98 us -> none  [the longest x1 8 us: per_device(): (returned[:, 0].astype(jnp.float32) + returned[:, 1].astype(jnp.float32))...]
    broadcast_in_dim x1 -> x0, local copies, waits for them, and re-layouts: 7.91 us -> none  [per_device(): jnp.broadcast_to(buffer.reshape(experts, 1, capacity, model_width), (expe...]
  transfers between devices with their start and end apart: 5 -> 5, of which waited for: 5 -> 5; matrix products, arithmetic and copies ran while one was open for 6% -> 7% of each run, Pallas kernels for 0% -> 0%
where the time goes in v1:
time: 404 us
  waiting for transfers between devices  171 us (42%)
  blocking collectives  121 us (30%)
  matrix products  63.5 us (16%)
  local copies, waits for them, and re-layouts  19.4 us (5%)
  between operations  13.8 us (3%)
  other arithmetic  11 us (3%)
    all_to_all x1, blocking collectives, per_device(): lax.all_to_all(sending, ('group', 'expert'), split_axis=0, concat_axis=0,...  121 us
    all_to_all x1, waiting for transfers between devices, per_device(): lax.all_to_all(combined.reshape(2 * experts, half_rows, model_width), ('g...  117 us
    all_gather x1, waiting for transfers between devices, per_device(): lax.all_gather(jnp.concatenate([cached_prefix_keys, cached_prefix_values]...  23.6 us
    dot_general x2, matrix products, half_expert(): jnp.dot(hidden_act, local_down, preferred_element_type=jnp.float32)  22.2 us
    all_gather x1, waiting for transfers between devices, per_device(): lax.all_gather(jnp.concatenate([suffix_key_rows, suffix_value_rows], axis...  20.8 us
    unnamed x44, local copies, waits for them, and re-layouts  11.9 us
    dot_general x2, matrix products, half_expert(): lax.dot_general(rows, local_up, (((1,), (1,)), ((), ())), preferred_eleme...  11.7 us
    ppermute x1, waiting for transfers between devices, per_device(): pair_rows = lax.ppermute(own_rows, 'expert', pairs)  8.66 us
  transfers between devices with their start and end apart: 5, of which 5 were waited for; matrix products, arithmetic and copies ran while one was open for 7% of the time, Pallas kernels for 0%

profile of v1, /device:TPU:0, one launch (start us, length us, event | category | flops | bytes accessed | tf_op | source)
XLA Modules:
  0.0 403.9 jit_solution(4623251032438831670)
XLA Ops:
  15.7 1.7 reduce-window.19
  21.1 23.6 %all-gather.3.cloned.1.call-done = bf16[1024,1024]{0,1:T(8,128)(2,1)} async-done(((bf16[128,1024]{0,1:T(8,128)(2,1)}), bf16[1024,1024]{0,1:T(8,128)(2,1)}) %all-gather.3.cloned.1.call-update) | async-done | bytes 2097168 | tf_op jit(solution)/shard_map/all_gather | solution.py:91
  44.7 2.8 fusion.72
  47.4 6.2 %bitcast_reduce_fusion = (f32[128,4,5]{0,2,1:T(8,128)S(1)}, f32[4,1024,128,5]{2,1,3,0:T(8,128)}) fusion(pred[128]{0:T(512)(128)(4,1)} %broadcast_compare_fusion, bf16[1024,4,128,1]{0,2,3,1:T(8,128)(2,1)S(1)} %bitcast.142, bf16[128,4,5,128]{0,3,2,1:T(8,128)(2,1)S(1)} %bitcast.135), kind=kOutput, calls=%fused_computation.2 | convolution fusion | flops 678950400 | bytes 12200064 | tf_op jit(solution)/shard_map/tkgd,skd->tkgs/dot_general | solution.py:63
  53.7 20.8 %all-gather.5.cloned.1.call-done = bf16[1024,1024]{0,1:T(8,128)(2,1)} async-done(((bf16[128,1024]{0,1:T(8,128)(2,1)}), bf16[1024,1024]{0,1:T(8,128)(2,1)}) %all-gather.5.cloned.1.call-update) | async-done | bytes 2097168 | tf_op jit(solution)/shard_map/all_gather | solution.py:97
  74.4 2.7 fusion.71
  77.1 1.6 fusion.2
  79.4 2.4 fusion.3
  82.0 2.4 fusion.5
  84.4 2.7 fusion.41
  87.1 3.0 divide_convert_fusion
  90.1 6.7 %multiply_reduce_fusion = (f32[128]{0:T(128)S(1)}, f32[128,2560]{1,0:T(8,128)S(1)}) fusion(bf16[128,2560]{0,1:T(8,128)(2,1)S(1)} %bitcast.143, bf16[2560,2560]{1,0:T(8,128)(2,1)} %param.23, bf16[128,2560]{1,0:T(8,128)(2,1)S(1)} %copy-done.6), kind=kOutput, calls=%fused_computation.47 | convolution fusion | flops 1679032192 | bytes 15729152 | tf_op jit(solution)/shard_map/dot_general | solution.py:116
  98.5 120.9 %all_to_all.10 = bf16[32,32,2560]{2,1,0:T(8,128)(2,1)S(1)} all-to-all(bf16[32,32,2560]{2,1,0:T(8,128)(2,1)S(1)} %bitcast.134), channel_id=1, replica_groups=mesh['group'=4,'expert'=8] {'group','expert'}, dimensions={0} | all-to-all | bytes 10485760 | tf_op jit(solution)/shard_map/all_to_all | solution.py:155
  219.4 2.3 copy-done.3
  221.7 8.7 %collective-permute-done = bf16[1024,2560]{1,0:T(8,128)(2,1)S(1)} collective-permute-done((bf16[1024,2560]{1,0:T(8,128)(2,1)S(1)}, bf16[1024,2560]{1,0:T(8,128)(2,1)S(1)}, u32[]{:S(2)}, u32[]{:S(2)}) %collective-permute-start) | collective-permute-done | bytes 5242912 | tf_op jit(solution)/shard_map/ppermute | solution.py:157
  230.4 2.4 copy-done.14
  232.8 4.2 %fusion.19 = f32[1024,512]{1,0:T(8,128)} fusion(bf16[1024,2560]{1,0:T(8,128)(2,1)S(1)} %collective-permute-done, bf16[1,512,2560]{2,1,0:T(8,128)(2,1)S(1)} %copy-done.15), kind=kOutput, calls=%fused_computation.31 | convolution fusion | flops 2684354560 | bytes 9961472 | tf_op jit(solution)/shard_map/dot_general | solution.py:146
  237.0 10.6 %convolution_convert_fusion = bf16[1024,2560]{1,0:T(8,128)(2,1)} fusion(bf16[1,512,2560]{2,1,0:T(8,128)(2,1)S(1)} %copy-done, f32[1024,512]{1,0:T(8,128)} %fusion.19, bf16[1024,2560]{1,0:T(8,128)(2,1)} %copy-done.14, bf16[1,512,2560]{2,1,0:T(8,128)(2,1)} %param.27), kind=kOutput, calls=%fused_computation.13 | convolution fusion | flops 5374476288 | bytes 17825792 | tf_op jit(solution)/shard_map/dot_general | solution.py:150
  247.7 7.5 %fusion.21 = f32[1024,512]{1,0:T(8,128)} fusion(bf16[1024,2560]{1,0:T(8,128)(2,1)} %bitcast.139, bf16[1,512,2560]{2,1,0:T(8,128)(2,1)} %param.28), kind=kOutput, calls=%fused_computation.33 | convolution fusion | flops 2684354560 | bytes 9961472 | tf_op jit(solution)/shard_map/dot_general | solution.py:146
  256.5 11.6 %add_convert_fusion = bf16[1024,2560]{1,0:T(8,128)(2,1)} fusion(bf16[1024,2560]{1,0:T(8,128)(2,1)} %collective-permute-done.1, bf16[1,512,2560]{2,1,0:T(8,128)(2,1)S(1)} %copy-done, f32[1024,512]{1,0:T(8,128)} %fusion.21, bf16[1024,2560]{1,0:T(8,128)(2,1)} %bitcast.140, bf16[1,512,2560]{2,1,0:T(8,128)(2,1)} %param.27), kind=kOutput, calls=%fused_computation.5 | convolution fusion | flops 5384962048 | bytes 23068672 | tf_op jit(solution)/shard_map/dot_general | solution.py:150
  268.1 3.7 all-to-all-start.1
  272.3 117.0 %all-to-all-done.1 = bf16[32,32,2560]{2,1,0:T(8,128)(2,1)} async-done(((bf16[32,32,2560]{2,1,0:T(8,128)(2,1)}), bf16[32,32,2560]{2,1,0:T(8,128)(2,1)}, u32[]{:S(2)}, u32[]{:S(2)}) %all-to-all-start.1) | async-done | bytes 5242912 | tf_op jit(solution)/shard_map/all_to_all | solution.py:164
  389.4 3.4 fusion.57
  392.8 4.3 %fusion.15 = bf16[128,2560]{1,0:T(8,128)(2,1)} fusion(f32[128,2560]{1,0:T(8,128)S(1)} %copy-done.2, f32[128,2560]{1,0:T(8,128)S(1)} %fusion.57, bf16[1024,2560]{1,0:T(8,128)(2,1)} %bitcast.26, f32[128,1024]{1,0:T(8,128)S(1)} %select_reduce_fusion), kind=kOutput, calls=%fused_computation.24 | convolution fusion | flops 672595968 | bytes 9043968 | tf_op jit(solution)/shard_map/dot_general | solution.py:182
  (79 shorter events, 16.9 us)
Async XLA Ops:
  6.5 230.4 %copy-start = (bf16[1,512,2560]{2,1,0:T(8,128)(2,1)S(1)}, bf16[1,512,2560]{2,1,0:T(8,128)(2,1)}, u32[]{:S(2)}) copy-start(bf16[1,512,2560]{2,1,0:T(8,128)(2,1)} %param.29) | copy-start | bytes 7864324
  6.5 38.1 %all-gather.3.cloned.1.call-start = ((), (), s32[]{:S(2)}) async-start(), calls=%async_computation.2 | async-start | bytes 2359296 | tf_op jit(solution)/shard_map/all_gather | solution.py:91
  9.5 65.0 %all-gather.5.cloned.1.call-start = ((), (), s32[]{:S(2)}) async-start(), calls=%async_computation.3 | async-start | bytes 2359296 | tf_op jit(solution)/shard_map/all_gather | solution.py:97
  19.7 0.6 copy-start.9
  77.1 4.8 %slice-start = ((s8[10485760]{0:T(1024)(128)(4,1)}), s8[4194304]{0:T(1024)(128)(4,1)S(1)}, s32[]{:S(2)}) async-start(s8[10485760]{0:T(1024)(128)(4,1)} %bitcast.132), calls=%async_computation.4 | async-start | bytes 8388608
  77.1 4.8 %slice-start.1 = ((s8[10485760]{0:T(1024)(128)(4,1)}), s8[4194304]{0:T(1024)(128)(4,1)S(1)}, s32[]{:S(2)}) async-start(s8[10485760]{0:T(1024)(128)(4,1)} %bitcast.132), calls=%async_computation.5 | async-start | bytes 8388608
  78.8 0.6 copy-start.7
  79.4 2.5 slice-start.2
  79.4 2.5 copy-start.13
  81.9 2.4 copy-start.8
  81.9 2.4 copy-start.4
  84.4 2.7 copy-start.5
  87.1 3.0 copy-start.6
  90.1 6.8 %copy-start.12 = (f32[2560]{0:T(1024)S(1)}, f32[2560]{0:T(1024)}, u32[]{:S(2)}) copy-start(f32[2560]{0:T(1024)} %param.24) | copy-start | bytes 30724
  96.8 1.6 copy-start.1
  98.5 134.3 %copy-start.15 = (bf16[1,512,2560]{2,1,0:T(8,128)(2,1)S(1)}, bf16[1,512,2560]{2,1,0:T(8,128)(2,1)}, u32[]{:S(2)}) copy-start(bf16[1,512,2560]{2,1,0:T(8,128)(2,1)} %param.28) | copy-start | bytes 7864324
  219.4 2.3 copy-start.3
  221.7 8.7 %collective-permute-start = (bf16[1024,2560]{1,0:T(8,128)(2,1)S(1)}, bf16[1024,2560]{1,0:T(8,128)(2,1)S(1)}, u32[]{:S(2)}, u32[]{:S(2)}) collective-permute-start(bf16[1024,2560]{1,0:T(8,128)(2,1)S(1)} %bitcast.138), channel_id=1, source_target_pairs={{0,1},{1,0},{2,3},{3,2},{4,5},{5,4},{6,7},{7,6},{8,9},{9,8},{10,11... | collective-permute-start | bytes 15728648 | tf_op jit(solution)/shard_map/ppermute | solution.py:157
  230.4 2.4 copy-start.14
  247.5 9.0 %collective-permute-start.1 = (bf16[1024,2560]{1,0:T(8,128)(2,1)}, bf16[1024,2560]{1,0:T(8,128)(2,1)}, u32[]{:S(2)}, u32[]{:S(2)}) collective-permute-start(bf16[1024,2560]{1,0:T(8,128)(2,1)} %convolution_convert_fusion), channel_id=1, source_target_pairs={{0,1},{1,0},{2,3},{3,2},{4,5},{5,4},{6,7},{7,6},{8,9},{9,8},{10,11... | collective-permute-start | bytes 15728648 | tf_op jit(solution)/shard_map/ppermute | solution.py:159
  268.1 3.7 copy-start.11
  268.1 3.8 copy-start.10
  268.1 121.2 %all-to-all-start.1 = ((bf16[32,32,2560]{2,1,0:T(8,128)(2,1)}), bf16[32,32,2560]{2,1,0:T(8,128)(2,1)}, u32[]{:S(2)}, u32[]{:S(2)}) async-start(bf16[32,32,2560]{2,1,0:T(8,128)(2,1)} %bitcast.141), calls=%async_computation.1 | async-start | bytes 10485760 | tf_op jit(solution)/shard_map/all_to_all | solution.py:164
  389.4 3.5 copy-start.2
Sparse Core Ops, SparseCore 0:
  9.6 35.0 all-gather.2
  46.3 28.1 all-gather.4
